TPU v7x, 32 devices: a whole 2x2x4 slice. The times are simulated.
32 devices in a mesh: section: 8 (over y, x, core), seq: 4 (over z).
Axes of the slice: x: 2, y: 2, z: 4, core: 2. Of those that a mesh axis runs over, the one named last changes fastest.
Arguments:
- grad_out: bfloat16 [8, 512, 2048], P('section', 'seq'), may hold values from -6 to 6
- block_input: bfloat16 [8, 512, 2048], P('section', 'seq'), may hold values from -5 to 5
- skip_saved: bfloat16 [8, 512, 2048], P('section', 'seq'), may hold values from -2 to 2
- saved_qkv: bfloat16 [8, 3, 512, 2048], P('section', None, None, 'seq'), may hold values from -16 to 16
- out_weight: bfloat16 [8, 2048, 2048], P('section', 'seq'), may hold values from -0.125 to 0.125
- qkv_weight: bfloat16 [8, 3, 2048, 2048], P('section', None, 'seq'), may hold values from -0.125 to 0.125
- gate: float32 [8, 2048], P('section'), may hold values from 0.5 to 1.5
- norm_scale: float32 [8, 2048], P('section'), may hold values from -0.5 to 0.5
- skip_gain: float32 [8, 2048], P('section'), may hold values from 0.3 to 1.5
Outputs:
- next_grad: bfloat16 [8, 512, 2048], P('section', 'seq')
- down_grad: bfloat16 [8, 512, 2048], P('section', 'seq')
- gain_grad: float32 [8, 2048], P('section')
All inputs are finite; a program needn't handle non-finite values.
Results may differ from a plain program's by a relative error of at most 0.015.
Values may be sent and summed in bfloat16 or wider, within the bound.
No kernel may reach another device: no remote copies, remote signals or barrier semaphores. Data moves between devices by JAX's collectives and lax.ppermute only.
A program may use at most 128 MiB of HBM per device.

v0:
```python
import jax
import jax.numpy as jnp
from jax import lax
from jax.sharding import PartitionSpec as P

HEAD_DIM = 128
norm_eps = 1e-06


def passed_along(block, axis, distance):
    devices = range(lax.axis_size(axis))
    route = [(i - distance, i) for i in devices if i - distance in devices]
    return lax.ppermute(block, axis, route)


def local_attention(query_all, keys_all, values_all, grad_cols, head_count, head_size):
    factor = head_size ** (-0.5)
    total_rows = query_all.shape[0]
    block_rows = min(512, total_rows)
    block_count = total_rows // block_rows
    query_out, keys_out, values_out = ([], [], [])
    for head_idx in range(head_count):
        lower = head_idx * head_size
        query_head = query_all[:, lower : lower + head_size]
        keys_head = keys_all[:, lower : lower + head_size]
        values_head = values_all[:, lower : lower + head_size]
        grad_head = grad_cols[lower : lower + head_size, :]
        query_blocks = query_head.reshape(block_count, block_rows, head_size)
        grad_blocks = jnp.moveaxis(grad_head.reshape(head_size, block_count, block_rows), 1, 0)

        def visit(carried, blocks):
            keys_acc, values_acc = carried
            query_blk, grad_blk = blocks
            scores = (
                jnp.einsum("qd,kd->qk", query_blk, keys_head, preferred_element_type=jnp.float32)
                * factor
            )
            scores = scores - jnp.max(scores, axis=-1, keepdims=True)
            weights = jnp.exp(scores)
            probs = weights / jnp.sum(weights, axis=-1, keepdims=True)
            dprobs = jnp.einsum(
                "dq,kd->qk", grad_blk, values_head, preferred_element_type=jnp.float32
            )
            delta = jnp.sum(probs * dprobs, axis=-1, keepdims=True)
            dscores = probs * (dprobs - delta)
            probs_low = probs.astype(jnp.bfloat16)
            dscores_low = dscores.astype(jnp.bfloat16)
            values_acc = values_acc + jnp.einsum(
                "qk,dq->kd", probs_low, grad_blk, preferred_element_type=jnp.float32
            )
            keys_acc = keys_acc + jnp.einsum(
                "qk,qd->kd", dscores_low, query_blk, preferred_element_type=jnp.float32
            )
            query_grad = (
                jnp.einsum("qk,kd->qd", dscores_low, keys_head, preferred_element_type=jnp.float32)
                * factor
            ).astype(jnp.bfloat16)
            return ((keys_acc, values_acc), query_grad)

        empty = jnp.zeros((total_rows, head_size), jnp.float32)
        (keys_acc, values_acc), query_grads = lax.scan(
            visit, (empty, empty), (query_blocks, grad_blocks)
        )
        query_out.append(query_grads.reshape(total_rows, head_size))
        keys_out.append((keys_acc * factor).astype(jnp.bfloat16))
        values_out.append(values_acc.astype(jnp.bfloat16))
    return (
        jnp.concatenate(query_out, axis=1),
        jnp.concatenate(keys_out, axis=1),
        jnp.concatenate(values_out, axis=1),
    )


def on_device(
    grad_out,
    block_input,
    skip_saved,
    saved_qkv,
    out_weight,
    qkv_weight,
    gate,
    norm_scale,
    skip_gain,
):
    seq_count = lax.axis_size("seq")
    incoming_gradient = grad_out[0]
    tok_rows, features = incoming_gradient.shape
    local_width = out_weight.shape[1]
    head_size = HEAD_DIM
    head_count = local_width // head_size
    feat_group = features // seq_count
    gated = (incoming_gradient.astype(jnp.float32) * gate[0]).astype(jnp.bfloat16)
    weight_out = out_weight[0]
    rows_in = lax.all_gather(gated, "seq", axis=0, tiled=True)
    row_count = rows_in.shape[0]
    terms = jnp.einsum(
        "rgs,hgs->ghr",
        rows_in.reshape(row_count, seq_count, feat_group),
        weight_out.reshape(local_width, seq_count, feat_group),
        preferred_element_type=jnp.float32,
    )
    rounded = lax.optimization_barrier(terms.astype(jnp.bfloat16))
    grad_cols = jnp.sum(rounded.astype(jnp.float32), axis=0).astype(jnp.bfloat16)
    query_grad, keys_grad, values_grad = local_attention(
        saved_qkv[0, 0], saved_qkv[0, 1], saved_qkv[0, 2], grad_cols, head_count, head_size
    )
    weight_qkv = qkv_weight[0]
    total = jnp.dot(query_grad, weight_qkv[0], preferred_element_type=jnp.float32)
    total = total + jnp.dot(keys_grad, weight_qkv[1], preferred_element_type=jnp.float32)
    total = total + jnp.dot(values_grad, weight_qkv[2], preferred_element_type=jnp.float32)
    normed_grad = lax.psum_scatter(
        total.astype(jnp.bfloat16), "seq", scatter_dimension=0, tiled=True
    ).astype(jnp.float32)
    xvalue = block_input[0].astype(jnp.float32)
    mean_x = jnp.mean(xvalue, axis=-1, keepdims=True)
    centered_input = xvalue - mean_x
    var_x = jnp.mean(centered_input * centered_input, axis=-1, keepdims=True)
    inverse_deviation = 1.0 / jnp.sqrt(var_x + norm_eps)
    normalized_input = centered_input * inverse_deviation
    scaled_gradient = normed_grad * (1.0 + norm_scale[0])
    input_gradient = incoming_gradient.astype(jnp.float32) + inverse_deviation * (
        scaled_gradient
        - jnp.mean(scaled_gradient, axis=-1, keepdims=True)
        - normalized_input * jnp.mean(scaled_gradient * normalized_input, axis=-1, keepdims=True)
    )
    hand_grad = input_gradient.astype(jnp.bfloat16)
    next_grad = passed_along(hand_grad, "section", 1)
    last_flag = jnp.where(
        lax.axis_index("section") == lax.axis_size("section") - 1, 1.0, 0.0
    ).astype(jnp.float32)
    down_grad = ((skip_gain[0] + last_flag) * input_gradient).astype(jnp.bfloat16)
    gain_local = jnp.sum(input_gradient * skip_saved[0].astype(jnp.float32), axis=0)
    gain_grad = lax.psum(gain_local, "seq")
    return (next_grad[None], down_grad[None], gain_grad[None])


def solution(mesh):
    placed = (
        P("section", "seq", None),
        P("section", "seq", None),
        P("section", "seq", None),
        P("section", None, None, "seq"),
        P("section", "seq", None),
        P("section", None, "seq", None),
        P("section", None),
        P("section", None),
        P("section", None),
    )
    return jax.shard_map(
        on_device,
        mesh=mesh,
        in_specs=placed,
        out_specs=(P("section", "seq", None), P("section", "seq", None), P("section", None)),
        check_vma=False,
    )
```

profile of v0, /device:TPU:0, one launch (start us, length us, event | category | flops | bytes accessed | tf_op | source)
XLA Modules:
  0.0 152.5 jit_solution(16319385925375333558)
XLA Ops:
  7.2 1.9 %fusion.29 = bf16[128,2048]{1,0:T(8,128)(2,1)} fusion(bf16[1,128,2048]{2,1,0:T(8,128)(2,1)} %param.9, f32[2048]{0:T(1024)} %bitcast.73), kind=kLoop, calls=%fused_computation.49 | loop fusion | flops 786432 | bytes 1056768 | tf_op jit(solution)/shard_map/convert_element_type | solution.py:92
  9.2 4.6 %reshape_squeeze.3 = bf16[512,4,512]{2,1,0:T(4,128)(2,1)} reshape(bf16[1,512,2048]{2,1,0:T(8,128)(2,1)} %param.13) | data formatting | bytes 4194304 | tf_op jit(solution)/shard_map/reshape;squeeze | solution.py:99
  13.8 0.9 slice_bitcast_fusion.2
  15.3 0.3 fusion.106
  15.8 0.3 fusion.107
  16.3 0.3 fusion.108
  16.8 41.7 %all-gather.2.cloned.1.call-done = bf16[512,2048]{1,0:T(8,128)(2,1)} async-done(((bf16[128,2048]{1,0:T(8,128)(2,1)}), bf16[512,2048]{1,0:T(8,128)(2,1)}) %all-gather.2.cloned.1.call-update) | async-done | bytes 2097168 | tf_op jit(solution)/shard_map/all_gather | solution.py:94
  58.5 3.9 %copy.16 = bf16[512,2048]{0,1:T(8,128)(2,1)} copy(bf16[512,2048]{1,0:T(8,128)(2,1)} %all-gather.2.cloned.1.call-done) | data formatting | bytes 4194304 | tf_op jit(solution)/shard_map/all_gather | solution.py:94
  62.5 5.1 %convert_bitcast_fusion = bf16[4,512,512]{1,2,0:T(8,128)(2,1)} fusion(bf16[512,4,512]{0,2,1:T(8,128)(2,1)} %bitcast.65, bf16[512,4,512]{2,1,0:T(4,128)(2,1)} %reshape_squeeze.3), kind=kOutput, calls=%fused_computation.11 | convolution fusion | flops 1074790400 | bytes 6291456 | tf_op jit(solution)/shard_map/rgs,hgs->ghr/dot_general | solution.py:96
  67.6 2.9 %reduce_sum.140 = bf16[512,512]{0,1:T(8,128)(2,1)} reduce(bf16[4,512,512]{1,2,0:T(8,128)(2,1)} %convert_bitcast_fusion, bf16[]{:T(256)} %constant.84.clone.1), dimensions={0}, to_apply=%region_4.5 | reduce | flops 786432 | bytes 2621442 | tf_op jit(solution)/shard_map/reduce_sum | solution.py:103
  70.4 1.7 %convolution_convert_fusion = bf16[512,128]{0,1:T(8,128)(2,1)S(1)} fusion(bf16[512,512]{0,1:T(8,128)(2,1)} %reduce_sum.140, f32[512,512]{0,1:T(8,128)} %copy-done, f32[512]{0:T(512)S(1)} %fusion.39, f32[512]{0:T(512)S(1)} %get-tuple-element.84), kind=kOutput, calls=%fused_computation.36 | convolution fusion | flops 67960832 | bytes 1314816 | tf_op jit(solution)/shard_map/while/body/eval_jaxpr/qk,dq->kd/dot_general | solution.py:48
  72.3 0.3 multiply_reduce_fusion
  72.9 0.7 copy-done.4
  74.3 0.4 convolution_convert_fusion.1
  74.6 0.3 multiply_reduce_fusion.1
  75.8 0.4 convolution_convert_fusion.2
  76.2 0.3 multiply_reduce_fusion.2
  76.5 0.4 convolution_convert_fusion.3
  76.9 0.3 multiply_reduce_fusion.3
  77.5 0.3 fusion.17
  79.1 0.8 slice-done.1
  79.9 1.3 fusion.3
  81.2 1.3 fusion.1
  82.5 2.8 %add_convert_fusion = bf16[512,2048]{1,0:T(8,128)(2,1)} fusion(f32[512,2048]{1,0:T(8,128)S(1)} %fusion.3, f32[512,2048]{1,0:T(8,128)S(1)} %fusion.1, bf16[1,3,512,2048]{3,2,1,0:T(8,128)(2,1)S(1)} %bitcast.67, bf16[512,128]{0,1:T(8,128)(2,1)S(1)} %convolution_convert_fusion, bf16[512,128]{0,1:T(8,128)(2,1)S(1)} %convolution_convert_fusion.1, ...), kind=kOutput, calls=%fused_computation | convolution fusion | flops 1078984704 | bytes 13107200 | tf_op jit(solution)/shard_map/dot_general | solution.py:110
  85.3 1.0 copy-done.2
  86.8 41.1 %reduce-scatter.2.cloned.1.call-done = bf16[128,2048]{1,0:T(8,128)(2,1)} async-done(((bf16[512,2048]{1,0:T(8,128)(2,1)}), bf16[128,2048]{1,0:T(8,128)(2,1)}) %reduce-scatter.2.cloned.1.call-update) | async-done | bytes 524304 | tf_op jit(solution)/shard_map/reduce_scatter | solution.py:111
  127.9 1.4 fusion.31
  129.3 1.8 %fusion.30 = (f32[2048]{0:T(1024)S(1)}, f32[128,2048]{1,0:T(8,128)S(1)}) fusion(bf16[1,128,2048]{2,1,0:T(8,128)(2,1)S(1)} %copy-done.9, f32[128]{0:T(128)S(1)} %get-tuple-element.116, f32[128]{0:T(128)S(1)} %broadcast_multiply_fusion.2, bf16[1,128,2048]{2,1,0:T(8,128)(2,1)S(1)} %copy-done.2, f32[128]{0:T(128)S(1)} %get-tuple-element.117, ...), kind=kLoop, calls=%fused_computation.51 | loop fusion | flops 3667968 | bytes 3164160 | tf_op jit(solution)/shard_map/reduce_sum | solution.py:132
  131.2 0.9 fusion.40
  132.1 1.4 collective-permute-start
  133.5 11.4 %psum.7 = f32[1,2048]{1,0:T(1,128)} all-reduce(f32[1,2048]{1,0:T(1,128)S(1)} %bitcast.72), channel_id=1, replica_groups=mesh['section'=8,'seq'=4] {'seq'}, use_global_device_ids=true, to_apply=%region_19.20 | all-reduce | flops 2048 | bytes 16384 | tf_op jit(solution)/shard_map/psum | solution.py:133
  144.9 0.8 copy.25
  (58 shorter events, 5.1 us)
Async XLA Ops:
  7.2 51.4 %all-gather.2.cloned.1.call-start = ((), (), s32[]{:S(2)}) async-start(), calls=%async_computation.1 | async-start | bytes 2621440 | tf_op jit(solution)/shard_map/all_gather | solution.py:94
  9.2 4.7 %copy-start.8 = (bf16[1,3,512,512]{3,2,1,0:T(8,128)(2,1)S(1)}, bf16[1,3,512,512]{3,2,1,0:T(8,128)(2,1)}, u32[]{:S(2)}) copy-start(bf16[1,3,512,512]{3,2,1,0:T(8,128)(2,1)} %param.12) | copy-start | bytes 4718596
  9.2 118.7 %reduce-scatter.2.cloned.1.call-start = ((), (), s32[]{:S(2)}) async-start(), calls=%async_computation.2 | async-start | bytes 2621440 | tf_op jit(solution)/shard_map/reduce_scatter | solution.py:111
  14.7 1.6 %copy-start.3 = (bf16[512,512]{1,0:T(8,128)(2,1)}, bf16[512,512]{1,0:T(8,128)(2,1)S(1)}, u32[]{:S(2)}) copy-start(bf16[512,512]{1,0:T(8,128)(2,1)S(1)} %get-tuple-element.71) | copy-start | bytes 1572868
  14.7 1.6 %copy-start.5 = (bf16[512,512]{1,0:T(8,128)(2,1)}, bf16[512,512]{1,0:T(8,128)(2,1)S(1)}, u32[]{:S(2)}) copy-start(bf16[512,512]{1,0:T(8,128)(2,1)S(1)} %get-tuple-element.81) | copy-start | bytes 1572868
  15.1 1.0 copy-start
  70.4 1.7 %copy-start.1 = (f32[512,512]{0,1:T(8,128)S(1)}, f32[512,512]{0,1:T(8,128)}, u32[]{:S(2)}) copy-start(f32[512,512]{0,1:T(8,128)} %copy-done) | copy-start | bytes 3145732
  70.4 1.7 %copy-start.10 = (bf16[512,512]{1,0:T(8,128)(2,1)S(1)}, bf16[512,512]{1,0:T(8,128)(2,1)}, u32[]{:S(2)}) copy-start(bf16[512,512]{1,0:T(8,128)(2,1)} %get-tuple-element.80) | copy-start | bytes 1572868
  70.4 1.9 %copy-start.11 = (bf16[512,512]{0,1:T(8,128)(2,1)S(1)}, bf16[512,512]{0,1:T(8,128)(2,1)}, u32[]{:S(2)}) copy-start(bf16[512,512]{0,1:T(8,128)(2,1)} %reduce_sum.140) | copy-start | bytes 1572868
  72.6 1.0 copy-start.4
  72.6 1.4 copy-start.6
  76.9 2.2 %slice-start = ((s8[6291456]{0:T(1024)(128)(4,1)}), s8[4194304]{0:T(1024)(128)(4,1)S(1)}, s32[]{:S(2)}) async-start(s8[6291456]{0:T(1024)(128)(4,1)} %bitcast.66), calls=%async_computation.3 | async-start | bytes 8388608
  77.2 2.6 %slice-start.1 = ((s8[6291456]{0:T(1024)(128)(4,1)}), s8[2097152]{0:T(1024)(128)(4,1)S(1)}, s32[]{:S(2)}) async-start(s8[6291456]{0:T(1024)(128)(4,1)} %bitcast.66), calls=%async_computation.4 | async-start | bytes 4194304
  85.3 1.0 copy-start.2
  85.3 1.5 copy-start.12
  85.3 1.5 %copy-start.13 = (f32[1,2048]{1,0:T(1,128)S(1)}, f32[1,2048]{1,0:T(1,128)}, u32[]{:S(2)}) copy-start(f32[1,2048]{1,0:T(1,128)} %param.17) | copy-start | bytes 24580
  85.3 44.0 %copy-start.7 = (bf16[1,128,2048]{2,1,0:T(8,128)(2,1)S(1)}, bf16[1,128,2048]{2,1,0:T(8,128)(2,1)}, u32[]{:S(2)}) copy-start(bf16[1,128,2048]{2,1,0:T(8,128)(2,1)} %param.9) | copy-start | bytes 1572868
  85.3 44.0 %copy-start.9 = (bf16[1,128,2048]{2,1,0:T(8,128)(2,1)S(1)}, bf16[1,128,2048]{2,1,0:T(8,128)(2,1)}, u32[]{:S(2)}) copy-start(bf16[1,128,2048]{2,1,0:T(8,128)(2,1)} %param.11) | copy-start | bytes 1572868
  132.1 12.8 %collective-permute-start = (bf16[128,2048]{1,0:T(8,128)(2,1)S(1)}, bf16[128,2048]{1,0:T(8,128)(2,1)S(1)}, u32[]{:S(2)}, u32[]{:S(2)}) collective-permute-start(bf16[128,2048]{1,0:T(8,128)(2,1)S(1)} %get-tuple-element.83), channel_id=1, source_target_pairs={{0,4},{4,8},{8,12},{12,16},{16,20},{20,24},{24,28},{1,5},{5,9},{9,... | collective-permute-start | bytes 1572872 | tf_op jit(solution)/shard_map/ppermute | solution.py:13
Sparse Core Ops, SparseCore 0:
  10.1 48.3 all-gather.1
  85.4 42.4 reduce-scatter.1
where the time goes:
time: 153 us
  waiting for transfers between devices  82.8 us (54%)
  matrix products  18.2 us (12%)
  between operations  14.3 us (9%)
  local copies, waits for them, and re-layouts  13 us (8%)
  other arithmetic  11.4 us (7%)
  blocking collectives  11.4 us (7%)
    all_gather x1, waiting for transfers between devices, on_device(): rows_in = lax.all_gather(gated, 'seq', axis=0, tiled=True)  41.7 us
    reduce_scatter x1, waiting for transfers between devices, on_device(): lax.psum_scatter(total.astype(jnp.bfloat16), 'seq', scatter_dimension=0,...  41.1 us
    psum x1, blocking collectives, on_device(): gain_grad = lax.psum(gain_local, 'seq')  11.4 us
    dot_general x1, matrix products, on_device(): jnp.einsum('rgs,hgs->ghr', rows_in.reshape(row_count, seq_count, feat_gro...  5.12 us
    another operation x1, local copies, waits for them, and re-layouts, on_device(): weight_out.reshape(local_width, seq_count, feat_group)  4.61 us
    all_gather x1, local copies, waits for them, and re-layouts, on_device(): rows_in = lax.all_gather(gated, 'seq', axis=0, tiled=True)  3.93 us
    unnamed x33, local copies, waits for them, and re-layouts  3.57 us
  transfers between devices with their start and end apart: 3, of which 2 were waited for; matrix products, arithmetic and copies ran while one was open for 5% of the time, Pallas kernels for 0%

commit v1 on v0

--- a/solution.py
+++ b/solution.py
@@ -5,6 +5,12 @@
 
 HEAD_DIM = 128
 norm_eps = 1e-06
+
+
+def expand_edges(matrix, pos_dim):
+    matrix = jnp.moveaxis(matrix, 0, pos_dim)
+    v1 = matrix.shape
+    return matrix.reshape(*v1[:pos_dim], v1[pos_dim] * v1[pos_dim + 1], *v1[pos_dim + 2 :])
 
 
 def passed_along(block, axis, distance):
@@ -91,7 +97,16 @@
     feat_group = features // seq_count
     gated = (incoming_gradient.astype(jnp.float32) * gate[0]).astype(jnp.bfloat16)
     weight_out = out_weight[0]
-    rows_in = lax.all_gather(gated, "seq", axis=0, tiled=True)
+    axis_total = lax.axis_size("seq")
+    block_list = tuple(((idx, (idx + 1) % axis_total) for idx in range(axis_total)))
+    shelf = [gated]
+    while len(shelf) < axis_total:
+        next_value = lax.ppermute(shelf[-1], "seq", block_list)
+        shelf.append(next_value)
+    ready = lax.axis_index("seq")
+    view_out = jnp.stack(shelf)
+    shelf = view_out[(ready - jnp.arange(axis_total)) % axis_total]
+    rows_in = expand_edges(shelf, 0)
     row_count = rows_in.shape[0]
     terms = jnp.einsum(
         "rgs,hgs->ghr",

time: 153 us -> 156 us (1.020)
  waiting for transfers between devices: 82.8 us -> 72.4 us
  local copies, waits for them, and re-layouts: 13 us -> 18.8 us
  other arithmetic: 11.4 us -> 15.4 us
  starting transfers between devices: 1.45 us -> 4.47 us
    all_gather x1 -> x0, waiting for transfers between devices: 41.7 us -> none  [on_device(): rows_in = lax.all_gather(gated, 'seq', axis=0, tiled=True)]
    ppermute x0 -> x3, waiting for transfers between devices: none -> 32.3 us  [on_device(): next_value = lax.ppermute(shelf[-1], 'seq', block_list)]
    another operation x0 -> x1, local copies, waits for them, and re-layouts: none -> 4.51 us  [on_device(): rows_in.reshape(row_count, seq_count, feat_group)]
    all_gather x1 -> x0, local copies, waits for them, and re-layouts: 3.93 us -> none  [on_device(): rows_in = lax.all_gather(gated, 'seq', axis=0, tiled=True)]
    gather x0 -> x1, local copies, waits for them, and re-layouts: none -> 3.6 us  [on_device(): shelf = view_out[(ready - jnp.arange(axis_total)) % axis_total]]
    ppermute x0 -> x3, starting transfers between devices: none -> 3.06 us  [on_device(): next_value = lax.ppermute(shelf[-1], 'seq', block_list)]
    another operation x0 -> x1, other arithmetic: none -> 2.91 us  [on_device(): view_out = jnp.stack(shelf)]
  transfers between devices with their start and end apart: 3 -> 5, of which waited for: 2 -> 4; matrix products, arithmetic and copies ran while one was open for 5% -> 7% of each run, Pallas kernels for 0% -> 0%
where the time goes in v1:
time: 156 us
  waiting for transfers between devices  72.4 us (46%)
  matrix products  18.9 us (12%)
  local copies, waits for them, and re-layouts  18.8 us (12%)
  other arithmetic  15.4 us (10%)
  between operations  14.3 us (9%)
  blocking collectives  11.4 us (7%)
  starting transfers between devices  4.47 us (3%)
    reduce_scatter x1, waiting for transfers between devices, on_device(): lax.psum_scatter(total.astype(jnp.bfloat16), 'seq', scatter_dimension=0,...  40 us
    ppermute x3, waiting for transfers between devices, on_device(): next_value = lax.ppermute(shelf[-1], 'seq', block_list)  32.3 us
    psum x1, blocking collectives, on_device(): gain_grad = lax.psum(gain_local, 'seq')  11.4 us
    dot_general x1, matrix products, on_device(): jnp.einsum('rgs,hgs->ghr', rows_in.reshape(row_count, seq_count, feat_gro...  5 us
    another operation x1, local copies, waits for them, and re-layouts, on_device(): rows_in.reshape(row_count, seq_count, feat_group)  4.51 us
    another operation x1, local copies, waits for them, and re-layouts, on_device(): weight_out.reshape(local_width, seq_count, feat_group)  4.5 us
    unnamed x33, local copies, waits for them, and re-layouts  3.93 us
    gather x1, local copies, waits for them, and re-layouts, on_device(): shelf = view_out[(ready - jnp.arange(axis_total)) % axis_total]  3.6 us
  transfers between devices with their start and end apart: 5, of which 4 were waited for; matrix products, arithmetic and copies ran while one was open for 7% of the time, Pallas kernels for 0%

profile of v1, /device:TPU:0, one launch (start us, length us, event | category | flops | bytes accessed | tf_op | source)
XLA Modules:
  0.0 155.7 jit_solution(4805847330519669015)
XLA Ops:
  7.2 1.9 %fusion.34 = bf16[128,2048]{1,0:T(8,128)(2,1)} fusion(bf16[1,128,2048]{2,1,0:T(8,128)(2,1)} %param.9, f32[2048]{0:T(1024)} %bitcast.77), kind=kLoop, calls=%fused_computation.54 | loop fusion | flops 786432 | bytes 1056768 | tf_op jit(solution)/shard_map/convert_element_type | solution.py:98
  9.2 3.1 %collective-permute-start = (bf16[128,2048]{1,0:T(8,128)(2,1)}, bf16[128,2048]{1,0:T(8,128)(2,1)}, u32[]{:S(2)}, u32[]{:S(2)}) collective-permute-start(bf16[128,2048]{1,0:T(8,128)(2,1)} %fusion.34), channel_id=1, source_target_pairs={{0,1},{1,2},{2,3},{3,0},{4,5},{5,6},{6,7},{7,4},{8,9},{9,10},{10,1... | collective-permute-start | bytes 1572872 | tf_op jit(solution)/shard_map/ppermute | solution.py:104
  12.2 2.3 %slice_bitcast_fusion.2 = (bf16[512,512]{1,0:T(8,128)(2,1)S(1)}, bf16[512,512]{1,0:T(8,128)(2,1)}, bf16[512,512]{1,0:T(8,128)(2,1)S(1)}) fusion(bf16[1,3,512,512]{3,2,1,0:T(8,128)(2,1)} %param.12), kind=kLoop, calls=%fused_computation.109 | loop fusion | bytes 3145728 | tf_op jit(solution)/shard_map/squeeze | solution.py:120
  15.3 0.5 copy-done
  16.5 9.9 %collective-permute-done = bf16[128,2048]{1,0:T(8,128)(2,1)} collective-permute-done((bf16[128,2048]{1,0:T(8,128)(2,1)}, bf16[128,2048]{1,0:T(8,128)(2,1)}, u32[]{:S(2)}, u32[]{:S(2)}) %collective-permute-start) | collective-permute-done | bytes 524320 | tf_op jit(solution)/shard_map/ppermute | solution.py:104
  26.5 1.3 fusion.117
  28.0 13.7 %collective-permute-done.1 = bf16[128,2048]{1,0:T(8,128)(2,1)} collective-permute-done((bf16[128,2048]{1,0:T(8,128)(2,1)}, bf16[128,2048]{1,0:T(8,128)(2,1)}, u32[]{:S(2)}, u32[]{:S(2)}) %collective-permute-start.1) | collective-permute-done | bytes 524320 | tf_op jit(solution)/shard_map/ppermute | solution.py:104
  41.7 4.5 %reshape_squeeze.3 = bf16[512,4,512]{2,1,0:T(4,128)(2,1)} reshape(bf16[1,512,2048]{2,1,0:T(8,128)(2,1)} %param.13) | data formatting | bytes 4194304 | tf_op jit(solution)/shard_map/reshape;squeeze | solution.py:114
  46.2 1.1 fusion.35
  47.3 8.7 %collective-permute-done.2 = bf16[128,2048]{1,0:T(8,128)(2,1)} collective-permute-done((bf16[128,2048]{1,0:T(8,128)(2,1)}, bf16[128,2048]{1,0:T(8,128)(2,1)}, u32[]{:S(2)}, u32[]{:S(2)}) %collective-permute-start.2) | collective-permute-done | bytes 524320 | tf_op jit(solution)/shard_map/ppermute | solution.py:104
  56.0 2.9 %pad_maximum_fusion = bf16[4,128,2048]{2,1,0:T(8,128)(2,1)} fusion(bf16[1,128,2048]{2,1,0:T(8,128)(2,1)} %bitcast.7, bf16[1,128,2048]{2,1,0:T(8,128)(2,1)} %bitcast.6, bf16[1,128,2048]{2,1,0:T(8,128)(2,1)} %bitcast.5, bf16[1,128,2048]{2,1,0:T(8,128)(2,1)S(1)} %fusion.35), kind=kLoop, calls=%fused_computation.2 | loop fusion | flops 3145728 | bytes 4194304 | tf_op jit(solution)/shard_map/stack | solution.py:107
  58.9 3.6 %gather_fusion = bf16[4,128,2048]{2,1,0:T(8,128)(2,1)} fusion(bf16[4,128,2048]{2,1,0:T(8,128)(2,1)} %pad_maximum_fusion, s32[1024]{0:T(1024)S(1)} %pad_clamp_fusion), kind=kCustom, calls=%fused_computation | custom fusion | bytes 4194320 | tf_op jit(solution)/shard_map/gather | solution.py:108
  62.5 4.5 %reshape_reshape.3 = bf16[512,4,512]{2,1,0:T(4,128)(2,1)} reshape(bf16[4,128,2048]{2,1,0:T(8,128)(2,1)} %gather_fusion) | data formatting | bytes 4194304 | tf_op jit(solution)/shard_map/reshape;reshape | solution.py:113
  67.0 5.0 %convert_bitcast_fusion = bf16[4,512,512]{1,2,0:T(8,128)(2,1)} fusion(bf16[512,4,512]{2,1,0:T(4,128)(2,1)} %reshape_squeeze.3, bf16[512,4,512]{2,1,0:T(4,128)(2,1)} %reshape_reshape.3), kind=kOutput, calls=%fused_computation.14 | convolution fusion | flops 1074790400 | bytes 6291456 | tf_op jit(solution)/shard_map/rgs,hgs->ghr/dot_general | solution.py:111
  72.0 2.9 %reduce_sum.140 = bf16[512,512]{0,1:T(8,128)(2,1)} reduce(bf16[4,512,512]{1,2,0:T(8,128)(2,1)} %convert_bitcast_fusion, bf16[]{:T(256)} %constant.104.clone.1), dimensions={0}, to_apply=%region_4.5 | reduce | flops 786432 | bytes 2621442 | tf_op jit(solution)/shard_map/reduce_sum | solution.py:118
  74.9 1.7 %convolution_convert_fusion = bf16[512,128]{1,0:T(8,128)(2,1)S(1)} fusion(bf16[512,512]{0,1:T(8,128)(2,1)} %reduce_sum.140, f32[512,512]{0,1:T(8,128)} %copy-done, f32[512]{0:T(512)S(1)} %fusion.45, f32[512]{0:T(512)S(1)} %get-tuple-element.84), kind=kOutput, calls=%fused_computation.41 | convolution fusion | flops 67960832 | bytes 1314816 | tf_op jit(solution)/shard_map/while/body/eval_jaxpr/qk,dq->kd/dot_general | solution.py:54
  77.4 0.7 copy-done.7
  78.4 0.3 fusion.20
  82.3 0.3 fusion.18
  83.3 0.3 fusion.17
  83.6 0.7 slice-done.1
  84.3 1.3 fusion.3
  85.6 1.3 fusion.1
  86.9 2.6 %add_convert_fusion = bf16[512,2048]{1,0:T(8,128)(2,1)} fusion(f32[512,2048]{1,0:T(8,128)S(1)} %fusion.3, f32[512,2048]{1,0:T(8,128)S(1)} %fusion.1, bf16[1,3,512,2048]{3,2,1,0:T(8,128)(2,1)S(1)} %bitcast.73, bf16[512,128]{1,0:T(8,128)(2,1)S(1)} %convolution_convert_fusion, bf16[512,128]{1,0:T(8,128)(2,1)S(1)} %convolution_convert_fusion.1, ...), kind=kOutput, calls=%fused_computation.1 | convolution fusion | flops 1078984704 | bytes 13107200 | tf_op jit(solution)/shard_map/dot_general | solution.py:125
  89.6 1.0 copy-done.2
  91.1 40.0 %reduce-scatter.2.cloned.1.call-done = bf16[128,2048]{1,0:T(8,128)(2,1)} async-done(((bf16[512,2048]{1,0:T(8,128)(2,1)}), bf16[128,2048]{1,0:T(8,128)(2,1)}) %reduce-scatter.2.cloned.1.call-update) | async-done | bytes 524304 | tf_op jit(solution)/shard_map/reduce_scatter | solution.py:126
  131.1 1.4 fusion.37
  132.5 1.8 %fusion.36 = (f32[2048]{0:T(1024)S(1)}, f32[128,2048]{1,0:T(8,128)S(1)}) fusion(bf16[1,128,2048]{2,1,0:T(8,128)(2,1)S(1)} %copy-done.8, f32[128]{0:T(128)S(1)} %get-tuple-element.116, f32[128]{0:T(128)S(1)} %broadcast_multiply_fusion.2, bf16[1,128,2048]{2,1,0:T(8,128)(2,1)S(1)} %copy-done.2, f32[128]{0:T(128)S(1)} %get-tuple-element.117, ...), kind=kLoop, calls=%fused_computation.57 | loop fusion | flops 3667968 | bytes 3164160 | tf_op jit(solution)/shard_map/reduce_sum | solution.py:147
  134.4 0.9 fusion.46
  135.3 1.4 collective-permute-start.3
  136.7 11.4 %psum.7 = f32[1,2048]{1,0:T(1,128)} all-reduce(f32[1,2048]{1,0:T(1,128)S(1)} %bitcast.80), channel_id=1, replica_groups=mesh['section'=8,'seq'=4] {'seq'}, use_global_device_ids=true, to_apply=%region_19.20 | all-reduce | flops 2048 | bytes 16384 | tf_op jit(solution)/shard_map/psum | solution.py:148
  148.1 0.8 copy.25
  (66 shorter events, 7.4 us)
Async XLA Ops:
  7.2 123.9 %reduce-scatter.2.cloned.1.call-start = ((), (), s32[]{:S(2)}) async-start(), calls=%async_computation.1 | async-start | bytes 2621440 | tf_op jit(solution)/shard_map/reduce_scatter | solution.py:126
  9.2 17.3 %collective-permute-start = (bf16[128,2048]{1,0:T(8,128)(2,1)}, bf16[128,2048]{1,0:T(8,128)(2,1)}, u32[]{:S(2)}, u32[]{:S(2)}) collective-permute-start(bf16[128,2048]{1,0:T(8,128)(2,1)} %fusion.34), channel_id=1, source_target_pairs={{0,1},{1,2},{2,3},{3,0},{4,5},{5,6},{6,7},{7,4},{8,9},{9,10},{10,1... | collective-permute-start | bytes 1572872 | tf_op jit(solution)/shard_map/ppermute | solution.py:104
  14.5 1.5 copy-start.4
  14.5 1.5 copy-start.6
  14.8 1.0 copy-start
  26.5 15.2 %collective-permute-start.1 = (bf16[128,2048]{1,0:T(8,128)(2,1)}, bf16[128,2048]{1,0:T(8,128)(2,1)}, u32[]{:S(2)}, u32[]{:S(2)}) collective-permute-start(bf16[128,2048]{1,0:T(8,128)(2,1)} %collective-permute-done), channel_id=1, source_target_pairs={{0,1},{1,2},{2,3},{3,0},{4,5},{5,6},{6,7},{7,4},{8,9},{9,10},{10,1... | collective-permute-start | bytes 1572872 | tf_op jit(solution)/shard_map/ppermute | solution.py:104
  41.7 14.3 %collective-permute-start.2 = (bf16[128,2048]{1,0:T(8,128)(2,1)}, bf16[128,2048]{1,0:T(8,128)(2,1)}, u32[]{:S(2)}, u32[]{:S(2)}) collective-permute-start(bf16[128,2048]{1,0:T(8,128)(2,1)} %collective-permute-done.1), channel_id=1, source_target_pairs={{0,1},{1,2},{2,3},{3,0},{4,5},{5,6},{6,7},{7,4},{8,9},{9,10},{10,1... | collective-permute-start | bytes 1572872 | tf_op jit(solution)/shard_map/ppermute | solution.py:104
  41.7 4.5 %copy-start.11 = (f32[1,2048]{1,0:T(1,128)S(1)}, f32[1,2048]{1,0:T(1,128)}, u32[]{:S(2)}) copy-start(f32[1,2048]{1,0:T(1,128)} %param.15) | copy-start | bytes 24580
  74.9 1.7 %copy-start.1 = (f32[512,512]{0,1:T(8,128)S(1)}, f32[512,512]{0,1:T(8,128)}, u32[]{:S(2)}) copy-start(f32[512,512]{0,1:T(8,128)} %copy-done) | copy-start | bytes 3145732
  74.9 1.7 %copy-start.9 = (bf16[512,512]{1,0:T(8,128)(2,1)S(1)}, bf16[512,512]{1,0:T(8,128)(2,1)}, u32[]{:S(2)}) copy-start(bf16[512,512]{1,0:T(8,128)(2,1)} %get-tuple-element.80) | copy-start | bytes 1572868
  74.9 1.9 %copy-start.10 = (bf16[512,512]{0,1:T(8,128)(2,1)S(1)}, bf16[512,512]{0,1:T(8,128)(2,1)}, u32[]{:S(2)}) copy-start(bf16[512,512]{0,1:T(8,128)(2,1)} %reduce_sum.140) | copy-start | bytes 1572868
  77.1 1.0 copy-start.7
  77.1 1.3 copy-start.5
  81.4 2.2 %slice-start = ((s8[6291456]{0:T(1024)(128)(4,1)}), s8[4194304]{0:T(1024)(128)(4,1)S(1)}, s32[]{:S(2)}) async-start(s8[6291456]{0:T(1024)(128)(4,1)} %bitcast.72), calls=%async_computation.2 | async-start | bytes 8388608
  81.7 2.6 %slice-start.1 = ((s8[6291456]{0:T(1024)(128)(4,1)}), s8[2097152]{0:T(1024)(128)(4,1)S(1)}, s32[]{:S(2)}) async-start(s8[6291456]{0:T(1024)(128)(4,1)} %bitcast.72), calls=%async_computation.3 | async-start | bytes 4194304
  89.5 1.0 copy-start.2
  89.5 1.5 copy-start.12
  89.5 1.5 copy-start.13
  89.5 43.0 %copy-start.3 = (bf16[1,128,2048]{2,1,0:T(8,128)(2,1)S(1)}, bf16[1,128,2048]{2,1,0:T(8,128)(2,1)}, u32[]{:S(2)}) copy-start(bf16[1,128,2048]{2,1,0:T(8,128)(2,1)} %param.9) | copy-start | bytes 1572868
  89.5 43.0 %copy-start.8 = (bf16[1,128,2048]{2,1,0:T(8,128)(2,1)S(1)}, bf16[1,128,2048]{2,1,0:T(8,128)(2,1)}, u32[]{:S(2)}) copy-start(bf16[1,128,2048]{2,1,0:T(8,128)(2,1)} %param.11) | copy-start | bytes 1572868
  135.3 12.8 %collective-permute-start.3 = (bf16[128,2048]{1,0:T(8,128)(2,1)S(1)}, bf16[128,2048]{1,0:T(8,128)(2,1)S(1)}, u32[]{:S(2)}, u32[]{:S(2)}) collective-permute-start(bf16[128,2048]{1,0:T(8,128)(2,1)S(1)} %get-tuple-element.83), channel_id=1, source_target_pairs={{0,4},{4,8},{8,12},{12,16},{16,20},{20,24},{24,28},{1,5},{5,9},{9,... | collective-permute-start | bytes 1572872 | tf_op jit(solution)/shard_map/ppermute | solution.py:19
Sparse Core Ops, SparseCore 0:
  89.7 41.3 reduce-scatter.1
